TPU v7x, 256 devices: a whole 4x4x8 slice. The times are simulated.
256 devices in a mesh: row: 32 (over z, y_lo, core), col: 8 (over y_hi, x).
Axes of the slice: x: 4, y: 4 (y_hi: 2, y_lo: 2; y = y_hi * 2 + y_lo), z: 8, core: 2. Of those that a mesh axis runs over, the one named last changes fastest.
Arguments:
- features: bfloat16 [32768, 128], P(('col', 'row')), may hold values from -96 to 96
- weight: bfloat16 [128, 256], replicated, may hold values from -0.5 to 0.5
- bias: float32 [256], replicated, may hold values from -3 to 3
- cotangent: bfloat16 [32768, 256], P(('row', 'col')), may hold values from -6 to 6
- tile_values: bfloat16 [32, 8, 256, 128, 128], P('row', 'col'), may hold values from 0 to 4, as said below
- tile_pos: int32 [32, 8, 2, 256], P('row', 'col'), may hold values from 0 to 31, as said below
- tile_count: int32 [32, 8], P('row', 'col'), may hold values from 0 to 256, as said below
- block_perm: int32 [256], replicated, may hold values from 0 to 255, as said below
Outputs:
- hidden: bfloat16 [32768, 256], P(('row', 'col'))
- weight_grad: float32 [128, 256], replicated
- bias_grad: float32 [256], replicated
Inputs may be any that keep to these rules, and one draw needn't show every extreme that they name: `tile_values`: entries are 0 or a weight of at least 0.25; slots t at or beyond tile_count[r, c] belong to no tile. `tile_pos`: entry [r, c, 0, t] is the slot's tile row, below 8, within row block r, and [r, c, 1, t] its tile column, below 32, within column block c, both in the reordered numbering; the slots of one cell hold distinct positions. `tile_count`: every draw has a cell with 256 live slots. `block_perm`: each aligned run of 8 entries is a permutation of that run's own indices.
All inputs are finite; a program needn't handle non-finite values.
Results may differ from a plain program's by a relative error of at most 0.0059.
Values may be sent and summed in bfloat16 or wider, within the bound.
No kernel may reach another device: no remote copies, remote signals or barrier semaphores. Data moves between devices by JAX's collectives and lax.ppermute only.
A program may use at most 64 MiB of HBM per device.

v0:
```python
import jax
import jax.numpy as jnp
from jax import lax
from jax.sharding import PartitionSpec as P


def local_index(block_perm, tile_axis, block_index, run_length):
    return jnp.take(block_perm, block_index * run_length + tile_axis) - block_index * run_length


def body(features, weight, bias, cotangent, tile_values, tile_pos, tile_count, block_perm):
    row_count = lax.axis_size("row")
    col_count = lax.axis_size("col")
    row_index = lax.axis_index("row")
    col_index = lax.axis_index("col")
    packed = tile_values[0, 0]
    positions = tile_pos[0, 0]
    live_count = tile_count[0, 0]
    max_tiles = packed.shape[0]
    tile_size = packed.shape[1]
    feat_width = features.shape[1]
    row_tiles = block_perm.shape[0] // row_count
    col_tiles = row_tiles * row_count // col_count
    block_tiles = min(64, max_tiles)
    lane_index = jnp.arange(block_tiles, dtype=jnp.int32)
    own_rows = local_index(block_perm, positions[0], row_index, row_tiles)
    own_cols = local_index(block_perm, positions[1], col_index, col_tiles)

    def degree_step(block_step, totals):
        row_acc, col_acc = totals
        slot_number = block_step * block_tiles + lane_index
        is_live = slot_number < live_count
        clamped = jnp.minimum(slot_number, max_tiles - 1)
        values = jnp.take(packed, clamped, axis=0).astype(jnp.float32)
        row_part = jnp.sum(values, axis=2)
        col_part = jnp.sum(values, axis=1)
        row_part = jnp.where(is_live[:, None], row_part, 0.0)
        col_part = jnp.where(is_live[:, None], col_part, 0.0)
        row_acc = row_acc.at[jnp.take(own_rows, clamped)].add(row_part)
        col_acc = col_acc.at[jnp.take(own_cols, clamped)].add(col_part)
        return (row_acc, col_acc)

    degree_blocks = (live_count + block_tiles - 1) // block_tiles
    row_acc, col_acc = lax.fori_loop(
        jnp.int32(0),
        degree_blocks,
        degree_step,
        (
            jnp.zeros((row_tiles, tile_size), jnp.float32),
            jnp.zeros((col_tiles, tile_size), jnp.float32),
        ),
    )
    col_part_flat = col_acc.reshape(col_tiles * tile_size)
    col_share = lax.psum_scatter(col_part_flat, "row", scatter_dimension=0, tiled=True)
    scaled = (lax.rsqrt(1.0 + col_share)[:, None] * features.astype(jnp.float32)).astype(
        jnp.bfloat16
    )
    gathered = lax.all_gather(scaled, "row", axis=0, tiled=True)
    feature_tiles = gathered.reshape(col_tiles, tile_size, feat_width)
    list_length = packed.shape[0]

    def product_step(block_step, partial_value):
        logical = block_step * block_tiles + lane_index
        is_live = logical < live_count
        is_upper = logical >= live_count
        source = jnp.where(is_upper, logical - live_count, logical)
        source = jnp.clip(source, 0, list_length - 1)
        slot_number = jnp.minimum(is_upper.astype(jnp.int32), 1 - 1)
        tile_block = jnp.take(packed, source, axis=0)
        tile_block = jnp.where(is_live[:, None, None], tile_block, jnp.zeros((), jnp.bfloat16))
        inputs = jnp.take(feature_tiles, jnp.take(own_cols, source), axis=0)
        products = jnp.einsum(
            "bpq,bqf->bpf", tile_block, inputs, preferred_element_type=jnp.float32
        )
        return partial_value.at[slot_number, jnp.take(own_rows, source)].add(products)

    product_blocks = (live_count + block_tiles - 1) // block_tiles
    initial = jnp.zeros((1, row_tiles, tile_size, feat_width), jnp.float32)
    partial_value = lax.fori_loop(jnp.int32(0), product_blocks, product_step, initial)
    own_sum = partial_value[0]
    row_part_flat = row_acc.reshape(row_tiles * tile_size)
    summed, degree_share = (
        lax.psum_scatter(
            own_sum.reshape(row_tiles * tile_size, feat_width),
            "col",
            scatter_dimension=0,
            tiled=True,
        ),
        lax.psum_scatter(row_part_flat, "col", scatter_dimension=0, tiled=True),
    )
    aggregated = (lax.rsqrt(1.0 + degree_share)[:, None] * summed).astype(jnp.bfloat16)
    preact = jnp.dot(aggregated, weight, preferred_element_type=jnp.float32) + bias
    logistic = jax.nn.sigmoid(preact)
    hidden = (preact * logistic).astype(jnp.bfloat16)
    preact_grad = (
        cotangent.astype(jnp.float32) * logistic * (1.0 + preact * (1.0 - logistic))
    ).astype(jnp.bfloat16)
    weight_part = jnp.einsum(
        "nf,nh->fh", aggregated, preact_grad, preferred_element_type=jnp.float32
    )
    bias_part = jnp.sum(preact_grad.astype(jnp.float32), axis=0)
    weight_sum, bias_sum = lax.psum((weight_part, bias_part), ("row", "col"))
    inverse_root = lax.rsqrt(jnp.float32(summed.shape[0] * row_count * col_count))
    return (hidden, weight_sum * inverse_root, bias_sum * inverse_root)


def solution(mesh):
    placed = (
        P(("col", "row"), None),
        P(),
        P(),
        P(("row", "col"), None),
        P("row", "col", None, None, None),
        P("row", "col", None, None),
        P("row", "col"),
        P(),
    )
    return jax.shard_map(
        body,
        mesh=mesh,
        in_specs=placed,
        out_specs=(P(("row", "col"), None), P(), P()),
        check_vma=False,
    )
```

profile of v0, /device:TPU:2, one launch (start us, length us, event | category | flops | bytes accessed | tf_op | source)
XLA Modules:
  0.0 723.7 jit_solution(14614431443404107920)
XLA Ops:
  7.9 0.8 slice_add_fusion
  8.7 2.0 gather_fusion.8
  10.7 2.0 gather_fusion.7
  12.7 9.5 %while.24 = (s32[]{:T(128)}, f32[8,128]{1,0:T(8,128)S(1)}, f32[32,128]{1,0:T(8,128)S(1)}, s32[]{:T(128)}, s32[256]{0:T(256)S(1)}, /*index=5*/s32[]{:T(128)}, bf1...) while((s32[]{:T(128)}, f32[8,128]{1,0:T(8,128)S(1)}, ...), condition=%wide.region_5.9_spmd.clone, body=%wide.region_0.8_spmd.clone.sunk | while | flops 4213635 | bytes 6451793 | solution.py:44
  12.8 0.7 compare_and_fusion.6
  13.4 0.8 gather_fusion.1
  14.2 0.8 gather_fusion
  15.0 4.3 gather_fusion.2
  19.4 0.9 convert_reduce_fusion.4
  20.2 1.0 scatter_custom_fusion.15
  21.2 1.0 scatter_custom_fusion.16
  22.2 122.7 %all-reduce.1 = f32[4096]{0:T(1024)S(1)} all-reduce(f32[4096]{0:T(1024)S(1)} %bitcast.44), channel_id=3, replica_groups=mesh['row'=32,'col'=8] {'row'}, use_global_device_ids=true, to_apply=%region_7.11.clone | all-reduce | flops 4096 | bytes 32768
  146.3 0.7 multiply_convert_fusion.3
  147.1 74.5 %all-gather.2.cloned.1.call-done = bf16[4096,128]{1,0:T(8,128)(2,1)} async-done(((bf16[128,128]{1,0:T(8,128)(2,1)}), bf16[4096,128]{1,0:T(8,128)(2,1)}) %all-gather.2.cloned.1.call-update) | async-done | bytes 1048592 | tf_op jit(solution)/shard_map/all_gather | solution.py:58
  221.6 24.0 %while.25 = (s32[]{:T(128)}, f32[1,8,128,128]{3,2,1,0:T(8,128)S(1)}, s32[]{:T(128)}, s32[]{:T(128)}, s32[256]{0:T(256)S(1)}, /*index=5*/bf16[256,128,128]{2,1,0:...) while((s32[]{:T(128)}, f32[1,8,128,128]{3,2,1,0:T(8,128)S(1)}, ...), condition=%wide.region_10.14_spmd.clone, body=%wide.region_8.13_spmd.clone.sunk | while | flops 272634240 | bytes 41956408 | solution.py:79
  221.6 0.7 compare_and_fusion.7
  222.4 0.8 gather_fusion.5
  223.2 0.8 gather_fusion.3
  224.0 0.7 fusion.44
  224.7 2.2 gather_fusion.6
  226.8 5.7 gather_fusion.4
  232.5 4.3 fusion.45
  236.8 8.8 %scatter_fusion = f32[8,128,128]{2,1,0:T(8,128)S(1)} fusion(f32[8,128,128]{2,1,0:T(8,128)S(1)} %bitcast.39, s32[64]{0:T(128)S(1)} %fusion.44, f32[64,128,128]{2,1,0:T(8,128)} %fusion.45), kind=kCustom, calls=%fused_computation.11.clone.clone.1 | custom fusion | flops 1048576 | bytes 12583168 | tf_op jit(solution)/shard_map/while/body/scatter-add | solution.py:75
  245.6 0.8 copy-done.1
  246.5 0.6 dynamic-slice
  247.7 43.6 %all-reduce = f32[1024]{0:T(1024)S(1)} all-reduce(f32[1024]{0:T(1024)S(1)} %bitcast.45), channel_id=2, replica_groups=mesh['row'=32,'col'=8] {'col'}, use_global_device_ids=true, to_apply=%region_6.10.clone | all-reduce | flops 1024 | bytes 8192
  291.4 102.7 %reduce-scatter.2.cloned.1.call-done = f32[128,128]{1,0:T(8,128)} async-done(((f32[1024,128]{1,0:T(8,128)}), f32[128,128]{1,0:T(8,128)}) %reduce-scatter.2.cloned.1.call-update) | async-done | bytes 65552 | tf_op jit(solution)/shard_map/reduce_scatter | solution.py:83
  394.1 1.7 convert_reduce_fusion.2
  395.8 73.9 %psum.15 = f32[256]{0:T(256)S(1)} all-reduce(f32[256]{0:T(256)S(1)} %get-tuple-element.182), channel_id=1, replica_groups=mesh['row'=32,'col'=8] {'row','col'}, use_global_device_ids=true, to_apply=%region_14.18 | all-reduce | flops 256 | bytes 2048 | tf_op jit(solution)/shard_map/psum | solution.py:102
  469.8 1.8 fusion.33
  472.1 243.5 %all-reduce.4.cloned.1.call-done = f32[128,256]{1,0:T(8,128)} async-done(((f32[128,256]{1,0:T(8,128)}), f32[128,256]{1,0:T(8,128)}) %all-reduce.4.cloned.1.call-update) | async-done | bytes 131088 | tf_op jit(solution)/shard_map/psum | solution.py:102
  715.6 1.6 broadcast_multiply_fusion
  (41 shorter events, 1.6 us)
Async XLA Ops:
  7.2 386.9 %copy-start = (bf16[128,256]{1,0:T(8,128)(2,1)S(1)}, bf16[128,256]{1,0:T(8,128)(2,1)}, u32[]{:S(2)}) copy-start(bf16[128,256]{1,0:T(8,128)(2,1)} %param.19) | copy-start | bytes 196612
  7.2 214.3 %all-gather.2.cloned.1.call-start = ((), (), s32[]{:S(2)}) async-start(), calls=%async_computation.1 | async-start | bytes 1081344 | tf_op jit(solution)/shard_map/all_gather | solution.py:58
  12.7 132.3 %copy-start.8 = (u32[256]{0:T(256)S(1)}, u32[256]{0:T(256)}, u32[]{:S(2)}) copy-start(u32[256]{0:T(256)} %constant.133) | copy-start | bytes 3076
  12.7 133.6 %copy-start.4 = (bf16[128,128]{1,0:T(8,128)(2,1)S(1)}, bf16[128,128]{1,0:T(8,128)(2,1)}, u32[]{:S(2)}) copy-start(bf16[128,128]{1,0:T(8,128)(2,1)} %param.18) | copy-start | bytes 98308
  12.7 381.4 %copy-start.5 = (bf16[128,256]{1,0:T(8,128)(2,1)S(1)}, bf16[128,256]{1,0:T(8,128)(2,1)}, u32[]{:S(2)}) copy-start(bf16[128,256]{1,0:T(8,128)(2,1)} %param.21) | copy-start | bytes 196612
  147.0 247.1 %reduce-scatter.2.cloned.1.call-start = ((), (), s32[]{:S(2)}) async-start(), calls=%async_computation.2 | async-start | bytes 589824 | tf_op jit(solution)/shard_map/reduce_scatter | solution.py:83
  221.6 24.9 %copy-start.7 = (u32[256]{0:T(256)S(1)}, u32[256]{0:T(256)}, u32[]{:S(2)}) copy-start(u32[256]{0:T(256)} %constant.129) | copy-start | bytes 3076
  221.6 172.5 %copy-start.6 = (f32[256]{0:T(256)S(1)}, f32[256]{0:T(256)}, u32[]{:S(2)}) copy-start(f32[256]{0:T(256)} %param.20) | copy-start | bytes 3076
  221.6 3.1 copy-start.2
  226.8 5.7 copy-start.3
  245.6 0.8 copy-start.1
  246.4 469.2 %all-reduce.4.cloned.1.call-start = ((), (), s32[]{:S(2)}) async-start(), calls=%async_computation.3 | async-start | bytes 262144 | tf_op jit(solution)/shard_map/psum | solution.py:102
Sparse Core Ops, SparseCore 0:
  147.1 74.3 all-gather.1
  246.6 147.4 reduce-scatter.1
  471.7 243.8 all-reduce.3
where the time goes:
time: 725 us; the launch traced here: 724 us
  waiting for transfers between devices  421 us (58%)
  blocking collectives  240 us (33%)
  local copies, waits for them, and re-layouts  21.3 us (3%)
  other arithmetic  17.5 us (2%)
  between operations  15.9 us (2%)
  matrix products  7.81 us (1%)
    psum x1, waiting for transfers between devices, body(): weight_sum, bias_sum = lax.psum((weight_part, bias_part), ('row', 'col'))  243 us
    unnamed x2, blocking collectives  166 us
    reduce_scatter x1, waiting for transfers between devices, body(): lax.psum_scatter(own_sum.reshape(row_tiles * tile_size, feat_width), 'col...  103 us
    all_gather x1, waiting for transfers between devices, body(): gathered = lax.all_gather(scaled, 'row', axis=0, tiled=True)  74.5 us
    psum x1, blocking collectives, body(): weight_sum, bias_sum = lax.psum((weight_part, bias_part), ('row', 'col'))  73.9 us
  transfers between devices with their start and end apart: 3, of which 3 were waited for; matrix products, arithmetic and copies ran while one was open for 0% of the time, Pallas kernels for 0%

commit v1 on v0

--- a/solution.py
+++ b/solution.py
@@ -99,7 +99,7 @@
         "nf,nh->fh", aggregated, preact_grad, preferred_element_type=jnp.float32
     )
     bias_part = jnp.sum(preact_grad.astype(jnp.float32), axis=0)
-    weight_sum, bias_sum = lax.psum((weight_part, bias_part), ("row", "col"))
+    weight_sum, bias_sum = lax.psum(lax.psum((weight_part, bias_part), "row"), "col")
     inverse_root = lax.rsqrt(jnp.float32(summed.shape[0] * row_count * col_count))
     return (hidden, weight_sum * inverse_root, bias_sum * inverse_root)
 

time: 725 us -> 703 us (0.970)
  waiting for transfers between devices: 421 us -> 396 us
    psum x1 -> x2, waiting for transfers between devices: 243 us -> 218 us  [the longest x1 131 us: body(): lax.psum((weight_part, bias_part), 'row')]
    psum x1 -> x2, blocking collectives: 73.9 us -> 74 us  [the longest x1 53.7 us: body(): lax.psum((weight_part, bias_part), 'row')]
  transfers between devices with their start and end apart: 3 -> 4, of which waited for: 3 -> 4; matrix products, arithmetic and copies ran while one was open for 0% -> 0% of each run, Pallas kernels for 0% -> 0%
where the time goes in v1:
time: 703 us; the launch traced here: 699 us
  waiting for transfers between devices  396 us (56%)
  blocking collectives  240 us (34%)
  local copies, waits for them, and re-layouts  21.3 us (3%)
  other arithmetic  17.5 us (2%)
  between operations  15.9 us (2%)
  matrix products  7.81 us (1%)
    unnamed x2, blocking collectives  166 us
    psum x1, waiting for transfers between devices, body(): lax.psum((weight_part, bias_part), 'row')  131 us
    reduce_scatter x1, waiting for transfers between devices, body(): lax.psum_scatter(own_sum.reshape(row_tiles * tile_size, feat_width), 'col...  103 us
    psum x1, waiting for transfers between devices, body(): lax.psum(lax.psum((weight_part, bias_part), 'row'), 'col')  87.3 us
    all_gather x1, waiting for transfers between devices, body(): gathered = lax.all_gather(scaled, 'row', axis=0, tiled=True)  74.5 us
    psum x1, blocking collectives, body(): lax.psum((weight_part, bias_part), 'row')  53.7 us
    psum x1, blocking collectives, body(): lax.psum(lax.psum((weight_part, bias_part), 'row'), 'col')  20.3 us
  transfers between devices with their start and end apart: 4, of which 4 were waited for; matrix products, arithmetic and copies ran while one was open for 0% of the time, Pallas kernels for 0%

profile of v1, /device:TPU:2, one launch (start us, length us, event | category | flops | bytes accessed | tf_op | source)
XLA Modules:
  0.0 698.9 jit_solution(10427341483074446523)
XLA Ops:
  7.9 0.8 slice_add_fusion
  8.7 2.0 gather_fusion.8
  10.7 2.0 gather_fusion.7
  12.7 9.5 %while.24 = (s32[]{:T(128)}, f32[8,128]{1,0:T(8,128)S(1)}, f32[32,128]{1,0:T(8,128)S(1)}, s32[]{:T(128)}, s32[256]{0:T(256)S(1)}, /*index=5*/s32[]{:T(128)}, bf1...) while((s32[]{:T(128)}, f32[8,128]{1,0:T(8,128)S(1)}, ...), condition=%wide.region_5.9_spmd.clone, body=%wide.region_0.8_spmd.clone.sunk | while | flops 4213635 | bytes 6451793 | solution.py:44
  12.8 0.7 compare_and_fusion.6
  13.4 0.8 gather_fusion.1
  14.2 0.8 gather_fusion
  15.0 4.3 gather_fusion.2
  19.4 0.9 convert_reduce_fusion.4
  20.2 1.0 scatter_custom_fusion.15
  21.2 1.0 scatter_custom_fusion.16
  22.2 122.7 %all-reduce.1 = f32[4096]{0:T(1024)S(1)} all-reduce(f32[4096]{0:T(1024)S(1)} %bitcast.44), channel_id=3, replica_groups=mesh['row'=32,'col'=8] {'row'}, use_global_device_ids=true, to_apply=%region_7.11.clone | all-reduce | flops 4096 | bytes 32768
  146.3 0.7 multiply_convert_fusion.3
  147.1 74.5 %all-gather.2.cloned.1.call-done = bf16[4096,128]{1,0:T(8,128)(2,1)} async-done(((bf16[128,128]{1,0:T(8,128)(2,1)}), bf16[4096,128]{1,0:T(8,128)(2,1)}) %all-gather.2.cloned.1.call-update) | async-done | bytes 1048592 | tf_op jit(solution)/shard_map/all_gather | solution.py:58
  221.6 24.0 %while.25 = (s32[]{:T(128)}, f32[1,8,128,128]{3,2,1,0:T(8,128)S(1)}, s32[]{:T(128)}, s32[]{:T(128)}, s32[256]{0:T(256)S(1)}, /*index=5*/bf16[256,128,128]{2,1,0:...) while((s32[]{:T(128)}, f32[1,8,128,128]{3,2,1,0:T(8,128)S(1)}, ...), condition=%wide.region_10.14_spmd.clone, body=%wide.region_8.13_spmd.clone.sunk | while | flops 272634240 | bytes 41956408 | solution.py:79
  221.6 0.7 compare_and_fusion.7
  222.4 0.8 gather_fusion.5
  223.2 0.8 gather_fusion.3
  224.7 2.2 gather_fusion.6
  226.8 5.7 gather_fusion.4
  232.5 4.3 fusion.45
  236.8 8.8 %scatter_fusion = f32[8,128,128]{2,1,0:T(8,128)S(1)} fusion(f32[8,128,128]{2,1,0:T(8,128)S(1)} %bitcast.39, s32[64]{0:T(128)S(1)} %fusion.44, f32[64,128,128]{2,1,0:T(8,128)} %fusion.45), kind=kCustom, calls=%fused_computation.11.clone.clone.1 | custom fusion | flops 1048576 | bytes 12583168 | tf_op jit(solution)/shard_map/while/body/scatter-add | solution.py:75
  245.6 0.8 copy-done.1
  247.7 43.6 %all-reduce = f32[1024]{0:T(1024)S(1)} all-reduce(f32[1024]{0:T(1024)S(1)} %bitcast.45), channel_id=2, replica_groups=mesh['row'=32,'col'=8] {'col'}, use_global_device_ids=true, to_apply=%region_6.10.clone | all-reduce | flops 1024 | bytes 8192
  291.4 102.7 %reduce-scatter.2.cloned.1.call-done = f32[128,128]{1,0:T(8,128)} async-done(((f32[1024,128]{1,0:T(8,128)}), f32[128,128]{1,0:T(8,128)}) %reduce-scatter.2.cloned.1.call-update) | async-done | bytes 65552 | tf_op jit(solution)/shard_map/reduce_scatter | solution.py:83
  394.1 1.7 convert_reduce_fusion.2
  395.8 1.8 fusion.33
  397.7 53.7 %psum.30 = f32[256]{0:T(256)S(1)} all-reduce(f32[256]{0:T(256)S(1)} %get-tuple-element.182), channel_id=1, replica_groups=mesh['row'=32,'col'=8] {'row'}, use_global_device_ids=true, to_apply=%region_15.19 | all-reduce | flops 256 | bytes 2048 | tf_op jit(solution)/shard_map/psum | solution.py:102
  451.4 20.3 %psum.31 = f32[256]{0:T(256)S(1)} all-reduce(f32[256]{0:T(256)S(1)} %psum.30), channel_id=1, replica_groups=mesh['row'=32,'col'=8] {'col'}, use_global_device_ids=true, to_apply=%region_16.20 | all-reduce | flops 256 | bytes 2048 | tf_op jit(solution)/shard_map/psum | solution.py:102
  471.7 131.2 %all-reduce.5.cloned.1.call-done = f32[128,256]{1,0:T(8,128)} async-done(((f32[128,256]{1,0:T(8,128)}), f32[128,256]{1,0:T(8,128)}) %all-reduce.5.cloned.1.call-update) | async-done | bytes 131088 | tf_op jit(solution)/shard_map/psum | solution.py:102
  603.4 87.3 %all-reduce.7.cloned.1.call-done = f32[128,256]{1,0:T(8,128)} async-done(((f32[128,256]{1,0:T(8,128)}), f32[128,256]{1,0:T(8,128)}) %all-reduce.7.cloned.1.call-update) | async-done | bytes 131088 | tf_op jit(solution)/shard_map/psum | solution.py:102
  690.7 1.6 broadcast_multiply_fusion
  (45 shorter events, 2.9 us)
Async XLA Ops:
  7.2 386.9 %copy-start = (bf16[128,256]{1,0:T(8,128)(2,1)S(1)}, bf16[128,256]{1,0:T(8,128)(2,1)}, u32[]{:S(2)}) copy-start(bf16[128,256]{1,0:T(8,128)(2,1)} %param.19) | copy-start | bytes 196612
  7.2 214.3 %all-gather.2.cloned.1.call-start = ((), (), s32[]{:S(2)}) async-start(), calls=%async_computation.1 | async-start | bytes 1081344 | tf_op jit(solution)/shard_map/all_gather | solution.py:58
  12.7 132.3 %copy-start.8 = (u32[256]{0:T(256)S(1)}, u32[256]{0:T(256)}, u32[]{:S(2)}) copy-start(u32[256]{0:T(256)} %constant.133) | copy-start | bytes 3076
  12.7 133.6 %copy-start.4 = (bf16[128,128]{1,0:T(8,128)(2,1)S(1)}, bf16[128,128]{1,0:T(8,128)(2,1)}, u32[]{:S(2)}) copy-start(bf16[128,128]{1,0:T(8,128)(2,1)} %param.18) | copy-start | bytes 98308
  12.7 381.4 %copy-start.5 = (bf16[128,256]{1,0:T(8,128)(2,1)S(1)}, bf16[128,256]{1,0:T(8,128)(2,1)}, u32[]{:S(2)}) copy-start(bf16[128,256]{1,0:T(8,128)(2,1)} %param.21) | copy-start | bytes 196612
  147.0 247.1 %reduce-scatter.2.cloned.1.call-start = ((), (), s32[]{:S(2)}) async-start(), calls=%async_computation.2 | async-start | bytes 589824 | tf_op jit(solution)/shard_map/reduce_scatter | solution.py:83
  221.6 24.9 %copy-start.7 = (u32[256]{0:T(256)S(1)}, u32[256]{0:T(256)}, u32[]{:S(2)}) copy-start(u32[256]{0:T(256)} %constant.129) | copy-start | bytes 3076
  221.6 172.5 %copy-start.6 = (f32[256]{0:T(256)S(1)}, f32[256]{0:T(256)}, u32[]{:S(2)}) copy-start(f32[256]{0:T(256)} %param.20) | copy-start | bytes 3076
  221.6 3.1 copy-start.2
  226.8 5.7 copy-start.3
  245.6 0.8 copy-start.1
  246.4 356.4 %all-reduce.5.cloned.1.call-start = ((), (), s32[]{:S(2)}) async-start(), calls=%async_computation.3 | async-start | bytes 262144 | tf_op jit(solution)/shard_map/psum | solution.py:102
  397.6 293.1 %all-reduce.7.cloned.1.call-start = ((), (), s32[]{:S(2)}) async-start(), calls=%async_computation.4 | async-start | bytes 262144 | tf_op jit(solution)/shard_map/psum | solution.py:102
Sparse Core Ops, SparseCore 0:
  147.1 74.3 all-gather.1
  246.6 147.4 reduce-scatter.1
  397.7 205.0 all-reduce.4
  605.3 85.4 all-reduce.6
